TPU v7x, 256 devices: a whole 4x4x8 slice. The times are simulated.
256 devices in a mesh: group: 8 (over y, core), dev: 32 (over z, x).
Axes of the slice: x: 4, y: 4, z: 8, core: 2. Of those that a mesh axis runs over, the one named last changes fastest.
Arguments:
- points: float32 [440, 131072], P(None, ('group', 'dev')), may hold values from -6 to 6
- residual: float32 [147, 131072], P(None, ('group', 'dev')), may hold values from -6 to 6
- coeffs: float32 [147, 131072], P(None, ('group', 'dev')), may hold values from -3 to 3
- owners: int32 [2], replicated, may hold values from 0 to 255
- offsets: int32 [2], replicated, may hold values from 0 to 256
Outputs:
- new_residual: float32 [147, 131072], P(None, ('group', 'dev'))
- new_coeffs: float32 [147, 131072], P(None, ('group', 'dev'))
All inputs are finite; a program needn't handle non-finite values.
Results may differ from a plain program's by a relative error of at most 0.0003.
Values sent between devices are 32-bit elements; how exact they have to be, the bound alone decides.
No kernel may reach another device: no remote copies, remote signals or barrier semaphores. Data moves between devices by JAX's collectives and lax.ppermute only.
A program may use at most 64 MiB of HBM per device.

v0:
```python
import jax
import jax.numpy as jnp
from jax import lax
from jax.sharding import PartitionSpec as P

BLOCK = 256
ridge = 2.0
step_norm = 1.5


def spread_2(value, axis, root):
    mine = lax.axis_index(axis) == root
    return lax.psum(jnp.where(mine, value, jnp.zeros_like(value)), axis)


def kernel_tile(cols, block):
    cross = lax.dot_general(
        block,
        cols,
        (((0,), (0,)), ((), ())),
        precision=lax.Precision.HIGHEST,
        preferred_element_type=jnp.float32,
    )
    dist = (
        jnp.sum(block * block, axis=0)[:, None]
        + jnp.sum(cols * cols, axis=0)[None, :]
        - 2.0 * cross
    )
    return jnp.exp(-dist / cols.shape[0])


def precondition(grad, block):
    gram = kernel_tile(block, block) + ridge * jnp.eye(block.shape[1], dtype=jnp.float32)
    lower = jnp.linalg.cholesky(gram)
    inner = lax.linalg.triangular_solve(lower, grad.T, left_side=True, lower=True)
    solved = lax.linalg.triangular_solve(lower, inner, left_side=True, lower=True, transpose_a=True)
    scale = step_norm / jnp.sqrt(jnp.mean(grad * grad) + 1e-06)
    return scale * solved.T


def contract(left, right):
    return lax.dot_general(
        left,
        right,
        (((1,), (1,)), ((), ())),
        precision=lax.Precision.HIGHEST,
        preferred_element_type=jnp.float32,
    )


def spread(delta, tile):
    return jnp.dot(delta, tile, precision=lax.Precision.HIGHEST, preferred_element_type=jnp.float32)


def body(points, residual, coeffs, owners, offsets):
    here = lax.axis_index(("group", "dev"))
    for step in range(2):
        local = lax.dynamic_slice_in_dim(points, offsets[step], BLOCK, 1)
        block = spread_2(local, ("group", "dev"), owners[step])
        tile = kernel_tile(points, block)
        grad = lax.psum(contract(residual, tile), ("group", "dev"))
        delta = precondition(grad, block)
        residual = residual - spread(delta, tile)
        current = lax.dynamic_slice_in_dim(coeffs, offsets[step], BLOCK, 1)
        mine = jnp.where(here == owners[step], delta, jnp.zeros_like(delta))
        coeffs = lax.dynamic_update_slice_in_dim(coeffs, current + mine, offsets[step], 1)
    return (residual, coeffs)


def solution(mesh):
    return jax.shard_map(
        body,
        mesh=mesh,
        in_specs=(
            P(None, ("group", "dev")),
            P(None, ("group", "dev")),
            P(None, ("group", "dev")),
            P(),
            P(),
        ),
        out_specs=(P(None, ("group", "dev")), P(None, ("group", "dev"))),
        check_vma=False,
    )
```

profile of v0, /device:TPU:1, one launch (start us, length us, event | category | flops | bytes accessed | tf_op | source)
XLA Modules:
  0.0 847.5 jit_solution(16834892905847499718)
XLA Ops:
  7.2 1.0 copy.40
  8.2 0.7 copy-done.7
  8.8 0.6 fusion.47
  12.0 0.6 copy-done.8
  12.7 0.7 fusion.46
  15.9 2.6 dynamic-slice_select_fusion
  18.7 256.7 %all-reduce.6.cloned.1.call-done = f32[440,256]{1,0:T(8,128)} async-done(((f32[440,256]{1,0:T(8,128)}), f32[440,256]{1,0:T(8,128)}) %all-reduce.6.cloned.1.call-update) | async-done | bytes 450576 | tf_op jit(solution)/shard_map/psum | solution.py:13
  275.4 1.2 multiply_reduce_fusion.2
  276.6 1.0 fusion.12
  277.6 0.1 copy.8
  277.8 11.7 %cholesky.130 = f32[128,128]{1,0:T(8,128)S(1)} custom-call(f32[128,128]{1,0:T(8,128)S(1)} %cholesky.194), custom_call_target="Cholesky" | custom-call | tf_op jit(solution)/shard_map/jit(cholesky)/cholesky | solution.py:34
  289.6 9.8 %custom-call.17 = f32[1,128,128]{1,2,0:T(8,128)S(1)} custom-call(f32[1,128,128]{2,1,0:T(8,128)S(1)} %get-tuple-element.68), custom_call_target="InvertDiagBlocksLowerTriangular" | custom-call | tf_op jit(solution)/shard_map/jit(cholesky)/cholesky | solution.py:34
  299.4 0.2 constant_dynamic-update-slice_fusion.1
  299.6 0.3 convolution_subtract_fusion.7
  299.9 11.7 %cholesky.147 = f32[128,128]{1,0:T(8,128)S(1)} custom-call(f32[128,128]{1,0:T(8,128)S(1)} %convolution_subtract_fusion.7), custom_call_target="Cholesky" | custom-call | tf_op jit(solution)/shard_map/jit(cholesky)/cholesky | solution.py:34
  311.6 12.0 %fusion.7 = f32[256,512]{1,0:T(8,128)S(1)} fusion(f32[440,256]{1,0:T(8,128)S(1)} %copy-done.2, f32[440,512]{1,0:T(8,128)S(1)} %copy-done, f32[512]{0:T(512)S(1)} %multiply_reduce_fusion, f32[256]{0:T(256)S(1)} %multiply_reduce_fusion.2), kind=kOutput, calls=%fused_computation.13 | convolution fusion | flops 692715520 | bytes 1879040 | tf_op jit(solution)/shard_map/dot_general | solution.py:17
  323.7 1.3 convolution_bitcast_fusion
  325.1 0.7 compare_reduce_fusion.2
  327.2 4.0 while.8
  327.2 0.6 fusion.79
  327.8 1.4 bitcast_dynamic-update-slice_fusion.4
  329.2 0.6 fusion.79
  329.8 1.4 bitcast_dynamic-update-slice_fusion.4
  331.2 19.7 %custom-call.19 = f32[2,128,128]{1,2,0:T(8,128)S(1)} custom-call(f32[2,128,128]{2,1,0:T(8,128)S(1)} %get-tuple-element.34), custom_call_target="InvertDiagBlocksLowerTriangular" | custom-call | tf_op jit(solution)/shard_map/triangular_solve/custom-call.4 | solution.py:36
  350.9 226.4 %all-reduce.10.cloned.1.call-done = (f32[147,256]{1,0:T(8,128)}, f32[440,256]{1,0:T(8,128)}) async-done(((f32[147,256]{1,0:T(8,128)}, f32[440,256]{1,0:T(8,128)}), (f32[147,256]{1,0:T(8,128)}, f32[440,256]{1,0:T(8,128)})) %all-reduce.10.cloned.1.call-update) | async-done | bytes 601104 | tf_op jit(solution)/shard_map/psum | solution.py:61
  577.3 1.2 multiply_reduce_fusion.1
  578.5 1.2 fusion.5
  579.7 1.0 fusion.17
  580.7 0.6 multiply_reduce_fusion.4
  581.3 0.3 fusion.22
  581.6 0.3 convolution_subtract_fusion.5
  581.9 0.3 fusion.33
  582.2 0.3 fusion.34
  582.5 0.3 convolution_subtract_fusion.4
  582.8 0.3 fusion.32
  583.8 0.5 convolution_subtract_fusion.1
  584.3 1.4 fusion.48
  585.6 0.1 copy.10
  585.8 11.7 %cholesky.164 = f32[128,128]{1,0:T(8,128)S(1)} custom-call(f32[128,128]{1,0:T(8,128)S(1)} %cholesky.197), custom_call_target="Cholesky" | custom-call | tf_op jit(solution)/shard_map/jit(cholesky)/cholesky | solution.py:34
  597.6 9.8 %custom-call.20 = f32[1,128,128]{1,2,0:T(8,128)S(1)} custom-call(f32[1,128,128]{2,1,0:T(8,128)S(1)} %get-tuple-element.64), custom_call_target="InvertDiagBlocksLowerTriangular" | custom-call | tf_op jit(solution)/shard_map/jit(cholesky)/cholesky | solution.py:34
  607.4 0.2 constant_dynamic-update-slice_fusion
  607.6 0.3 convolution_subtract_fusion.6
  607.9 11.9 %cholesky.181 = f32[128,128]{1,0:T(8,128)S(1)} custom-call(f32[128,128]{1,0:T(8,128)S(1)} %convolution_subtract_fusion.6), custom_call_target="Cholesky" | custom-call | tf_op jit(solution)/shard_map/jit(cholesky)/cholesky | solution.py:34
  619.8 0.7 compare_reduce_fusion
  621.9 4.0 while.9
  621.9 0.6 fusion.80
  622.5 1.4 bitcast_dynamic-update-slice_fusion.5
  623.9 0.6 fusion.80
  624.4 1.4 bitcast_dynamic-update-slice_fusion.5
  625.8 19.7 %custom-call.22 = f32[2,128,128]{1,2,0:T(8,128)S(1)} custom-call(f32[2,128,128]{2,1,0:T(8,128)S(1)} %get-tuple-element.36), custom_call_target="InvertDiagBlocksLowerTriangular" | custom-call | tf_op jit(solution)/shard_map/triangular_solve/custom-call.4 | solution.py:36
  645.5 0.1 bitcast_add_fusion.3
  645.6 1.5 dynamic_update_slice.6
  647.1 185.8 %all-reduce.8.cloned.1.call-done = f32[147,256]{1,0:T(8,128)} async-done(((f32[147,256]{1,0:T(8,128)}), f32[147,256]{1,0:T(8,128)}) %all-reduce.8.cloned.1.call-update) | async-done | bytes 150544 | tf_op jit(solution)/shard_map/psum | solution.py:61
  832.9 1.2 fusion.20
  834.2 0.3 convolution_subtract_fusion.3
  834.5 0.3 fusion.36
  834.8 0.3 fusion.37
  835.1 0.3 convolution_subtract_fusion.2
  835.4 0.3 fusion.35
  835.7 0.6 multiply_reduce_fusion.3
  837.0 1.2 convolution_subtract_fusion
  838.2 0.1 bitcast_add_fusion.2
  838.3 1.5 dynamic_update_slice.7
  839.8 0.7 copy-done.4
  (42 shorter events, 0.8 us)
Async XLA Ops:
  7.2 268.3 %all-reduce.6.cloned.1.call-start = ((), (), s32[]{:S(2)}) async-start(), calls=%async_computation | async-start | bytes 901120 | tf_op jit(solution)/shard_map/psum | solution.py:13
  8.2 0.7 copy-start.7
  12.0 0.7 copy-start.8
  15.9 2.7 copy-start
  18.5 558.8 %all-reduce.10.cloned.1.call-start = ((), (), s32[]{:S(2)}) async-start(), calls=%async_computation.2 | async-start | bytes 1212416 | tf_op jit(solution)/shard_map/psum | solution.py:61
  275.4 1.2 copy-start.2
  311.6 12.0 %copy-start.3 = (f32[147,512]{1,0:T(8,128)S(1)}, f32[147,512]{1,0:T(8,128)}, u32[]{:S(2)}) copy-start(f32[147,512]{1,0:T(8,128)} %param.11) | copy-start | bytes 903172
  325.0 507.9 %all-reduce.8.cloned.1.call-start = ((), (), s32[]{:S(2)}) async-start(), calls=%async_computation.1 | async-start | bytes 311296 | tf_op jit(solution)/shard_map/psum | solution.py:61
  577.3 1.2 copy-start.1
  579.6 1.0 copy-start.6
  832.9 1.2 copy-start.5
  839.8 0.7 copy-start.4
Sparse Core Ops, SparseCore 0:
  18.7 256.7 all-reduce.5
  325.1 252.1 all-reduce.9
  585.8 247.1 all-reduce.7
where the time goes:
time: 857 us; the launch traced here: 847 us
  waiting for transfers between devices  669 us (78%)
  other arithmetic  114 us (13%)
  matrix products  24.9 us (3%)
  between operations  23.6 us (3%)
  local copies, waits for them, and re-layouts  15.5 us (2%)
    psum x2, waiting for transfers between devices, body(): grad = lax.psum(contract(residual, tile), ('group', 'dev'))  412 us
    psum x1, waiting for transfers between devices, spread_2(): return lax.psum(jnp.where(mine, value, jnp.zeros_like(value)), axis)  257 us
    another operation x12, other arithmetic, precondition(): lower = jnp.linalg.cholesky(gram)  68.2 us
    another operation x5, other arithmetic, precondition(): lax.linalg.triangular_solve(lower, inner, left_side=True, lower=True, tra...  39.4 us
  transfers between devices with their start and end apart: 3, of which 3 were waited for; matrix products, arithmetic and copies ran while one was open for 10% of the time, Pallas kernels for 0%

commit v1 on v0

--- a/solution.py
+++ b/solution.py
@@ -58,7 +58,7 @@
         local = lax.dynamic_slice_in_dim(points, offsets[step], BLOCK, 1)
         block = spread_2(local, ("group", "dev"), owners[step])
         tile = kernel_tile(points, block)
-        grad = lax.psum(contract(residual, tile), ("group", "dev"))
+        grad = lax.psum(lax.psum(contract(residual, tile), "group"), "dev")
         delta = precondition(grad, block)
         residual = residual - spread(delta, tile)
         current = lax.dynamic_slice_in_dim(coeffs, offsets[step], BLOCK, 1)

time: 857 us -> 756 us (0.88)
  waiting for transfers between devices: 669 us -> 576 us
  matrix products: 24.9 us -> 15 us
    psum x2 -> x4, waiting for transfers between devices: 412 us -> 317 us  [body(): grad = lax.psum(lax.psum(contract(residual, tile), 'group'), 'dev')]
    dot_general x4, matrix products: 15.2 us -> 4.37 us  [kernel_tile(): lax.dot_general(block, cols, (((0,), (0,)), ((), ())), precision=lax.Prec...]
  transfers between devices with their start and end apart: 3 -> 5, of which waited for: 3 -> 4; matrix products, arithmetic and copies ran while one was open for 10% -> 16% of each run, Pallas kernels for 0% -> 0%
where the time goes in v1:
time: 756 us; the launch traced here: 748 us
  waiting for transfers between devices  576 us (76%)
  other arithmetic  114 us (15%)
  between operations  23.6 us (3%)
  local copies, waits for them, and re-layouts  18.6 us (2%)
  matrix products  15 us (2%)
    psum x4, waiting for transfers between devices, body(): grad = lax.psum(lax.psum(contract(residual, tile), 'group'), 'dev')  317 us
    psum x1, waiting for transfers between devices, spread_2(): return lax.psum(jnp.where(mine, value, jnp.zeros_like(value)), axis)  259 us
    another operation x12, other arithmetic, precondition(): lower = jnp.linalg.cholesky(gram)  68 us
    another operation x5, other arithmetic, precondition(): lax.linalg.triangular_solve(lower, inner, left_side=True, lower=True, tra...  40.2 us
  transfers between devices with their start and end apart: 5, of which 4 were waited for; matrix products, arithmetic and copies ran while one was open for 16% of the time, Pallas kernels for 0%

profile of v1, /device:TPU:1, one launch (start us, length us, event | category | flops | bytes accessed | tf_op | source)
XLA Modules:
  0.0 748.3 jit_solution(15869237270471446427)
XLA Ops:
  7.2 1.0 copy.42
  8.2 0.7 copy-done.10
  8.8 0.6 fusion.47
  12.0 0.6 copy-done.11
  12.7 0.7 fusion.46
  15.9 2.6 dynamic-slice_select_fusion
  18.5 1.1 copy-done
  19.7 259.5 %all-reduce.16.cloned.1.call-done = (f32[440,256]{1,0:T(8,128)}, f32[440,256]{1,0:T(8,128)}) async-done(((f32[440,256]{1,0:T(8,128)}, f32[440,256]{1,0:T(8,128)}), (f32[440,256]{1,0:T(8,128)}, f32[440,256]{1,0:T(8,128)})) %all-reduce.16.cloned.1.call-update) | async-done | bytes 901136 | tf_op jit(solution)/shard_map/psum | solution.py:13
  279.2 1.2 multiply_reduce_fusion.2
  280.4 1.0 fusion.12
  281.4 1.2 fusion.7
  282.6 1.3 convolution_bitcast_fusion
  284.0 0.5 all-reduce.10.cloned.1.call-start
  284.7 11.7 %cholesky.130 = f32[128,128]{1,0:T(8,128)S(1)} custom-call(f32[128,128]{1,0:T(8,128)S(1)} %cholesky.194), custom_call_target="Cholesky" | custom-call | tf_op jit(solution)/shard_map/jit(cholesky)/cholesky | solution.py:34
  296.5 9.8 %custom-call.17 = f32[1,128,128]{1,2,0:T(8,128)S(1)} custom-call(f32[1,128,128]{2,1,0:T(8,128)S(1)} %get-tuple-element.68), custom_call_target="InvertDiagBlocksLowerTriangular" | custom-call | tf_op jit(solution)/shard_map/jit(cholesky)/cholesky | solution.py:34
  306.5 0.3 convolution_subtract_fusion.7
  306.8 11.7 %cholesky.147 = f32[128,128]{1,0:T(8,128)S(1)} custom-call(f32[128,128]{1,0:T(8,128)S(1)} %convolution_subtract_fusion.7), custom_call_target="Cholesky" | custom-call | tf_op jit(solution)/shard_map/jit(cholesky)/cholesky | solution.py:34
  318.5 0.7 compare_reduce_fusion.2
  320.6 4.0 while.8
  320.6 0.6 fusion.79
  321.3 1.3 bitcast_dynamic-update-slice_fusion.4
  322.6 0.6 fusion.79
  323.3 1.3 bitcast_dynamic-update-slice_fusion.4
  324.6 20.4 %custom-call.19 = f32[2,128,128]{1,2,0:T(8,128)} custom-call(f32[2,128,128]{2,1,0:T(8,128)S(1)} %get-tuple-element.34), custom_call_target="InvertDiagBlocksLowerTriangular" | custom-call | tf_op jit(solution)/shard_map/triangular_solve/custom-call.4 | solution.py:36
  345.2 1.0 fusion.17
  346.4 0.7 copy-done.5
  347.1 11.7 %cholesky.164 = f32[128,128]{1,0:T(8,128)S(1)} custom-call(f32[128,128]{1,0:T(8,128)S(1)} %cholesky.197), custom_call_target="Cholesky" | custom-call | tf_op jit(solution)/shard_map/jit(cholesky)/cholesky | solution.py:34
  358.9 9.8 %custom-call.20 = f32[1,128,128]{1,2,0:T(8,128)S(1)} custom-call(f32[1,128,128]{2,1,0:T(8,128)S(1)} %get-tuple-element.64), custom_call_target="InvertDiagBlocksLowerTriangular" | custom-call | tf_op jit(solution)/shard_map/jit(cholesky)/cholesky | solution.py:34
  368.9 0.3 convolution_subtract_fusion.6
  369.2 11.7 %cholesky.181 = f32[128,128]{1,0:T(8,128)S(1)} custom-call(f32[128,128]{1,0:T(8,128)S(1)} %convolution_subtract_fusion.6), custom_call_target="Cholesky" | custom-call | tf_op jit(solution)/shard_map/jit(cholesky)/cholesky | solution.py:34
  380.9 0.7 compare_reduce_fusion
  383.0 0.3 all-reduce.12.cloned.1.call-start
  383.3 1.2 fusion.5
  384.5 135.9 %all-reduce.10.cloned.1.call-done = f32[147,256]{1,0:T(8,128)} async-done(((f32[147,256]{1,0:T(8,128)}), f32[147,256]{1,0:T(8,128)}) %all-reduce.10.cloned.1.call-update) | async-done | bytes 150544 | tf_op jit(solution)/shard_map/psum | solution.py:61
  520.3 1.2 fusion.22
  521.6 0.3 convolution_subtract_fusion.5
  521.9 0.6 copy-done.9
  522.5 0.3 fusion.33
  522.8 0.3 fusion.34
  523.1 0.3 convolution_subtract_fusion.4
  523.4 0.3 fusion.32
  523.7 0.6 multiply_reduce_fusion.4
  525.0 0.5 convolution_subtract_fusion.1
  525.5 1.4 fusion.48
  527.0 65.5 %all-reduce.12.cloned.1.call-done = f32[147,256]{1,0:T(8,128)} async-done(((f32[147,256]{1,0:T(8,128)}), f32[147,256]{1,0:T(8,128)}) %all-reduce.12.cloned.1.call-update) | async-done | bytes 150544 | tf_op jit(solution)/shard_map/psum | solution.py:61
  592.5 0.6 copy-done.13
  593.1 4.0 while.9
  593.1 0.6 fusion.80
  593.7 1.4 bitcast_dynamic-update-slice_fusion.5
  595.1 0.6 fusion.80
  595.7 1.4 bitcast_dynamic-update-slice_fusion.5
  597.1 19.7 %custom-call.22 = f32[2,128,128]{1,2,0:T(8,128)S(1)} custom-call(f32[2,128,128]{2,1,0:T(8,128)S(1)} %get-tuple-element.36), custom_call_target="InvertDiagBlocksLowerTriangular" | custom-call | tf_op jit(solution)/shard_map/triangular_solve/custom-call.4 | solution.py:36
  616.9 1.5 dynamic_update_slice.6
  618.4 115.5 %all-reduce.14.cloned.1.call-done = f32[147,256]{1,0:T(8,128)} async-done(((f32[147,256]{1,0:T(8,128)}), f32[147,256]{1,0:T(8,128)}) %all-reduce.14.cloned.1.call-update) | async-done | bytes 150544 | tf_op jit(solution)/shard_map/psum | solution.py:61
  733.9 1.2 fusion.20
  735.2 0.3 convolution_subtract_fusion.3
  735.5 0.3 fusion.36
  735.8 0.3 fusion.37
  736.1 0.3 convolution_subtract_fusion.2
  736.4 0.3 fusion.35
  736.7 0.6 multiply_reduce_fusion.3
  738.0 1.2 convolution_subtract_fusion
  739.3 1.5 dynamic_update_slice.7
  740.8 0.7 copy-done.4
  (58 shorter events, 1.8 us)
Async XLA Ops:
  7.2 272.0 %all-reduce.16.cloned.1.call-start = ((), (), s32[]{:S(2)}) async-start(), calls=%async_computation.4 | async-start | bytes 1802240 | tf_op jit(solution)/shard_map/psum | solution.py:13
  8.2 0.7 copy-start.10
  12.0 0.7 copy-start.11
  18.5 1.2 copy-start
  18.5 364.5 %all-reduce.8.cloned.1.call-start = ((), (), s32[]{:S(2)}) async-start(), calls=%async_computation | async-start | bytes 311296 | tf_op jit(solution)/shard_map/psum | solution.py:61
  279.2 1.2 copy-start.2
  281.4 1.2 copy-start.3
  284.0 236.4 %all-reduce.10.cloned.1.call-start = ((), (), s32[]{:S(2)}) async-start(), calls=%async_computation.1 | async-start | bytes 311296 | tf_op jit(solution)/shard_map/psum | solution.py:61
  320.5 24.6 %copy-start.1 = (f32[440,256]{1,0:T(8,128)S(1)}, f32[440,256]{1,0:T(8,128)}, u32[]{:S(2)}) copy-start(f32[440,256]{1,0:T(8,128)} %get-tuple-element.54) | copy-start | bytes 1351684
  324.6 20.5 %copy-start.12 = (s32[2,2]{1,0:T(2,128)}, s32[2,2]{1,0:T(2,128)S(1)}, u32[]{:S(2)}) copy-start(s32[2,2]{1,0:T(2,128)S(1)} %get-tuple-element.197) | copy-start | bytes 52
  346.4 0.7 copy-start.5
  347.1 21.6 %copy-start.6 = (f32[256,256]{1,0:T(8,128)S(1)}, f32[256,256]{1,0:T(8,128)}, u32[]{:S(2)}) copy-start(f32[256,256]{1,0:T(8,128)} %copy-done.5) | copy-start | bytes 786436
  383.0 209.4 %all-reduce.12.cloned.1.call-start = ((), (), s32[]{:S(2)}) async-start(), calls=%async_computation.2 | async-start | bytes 311296 | tf_op jit(solution)/shard_map/psum | solution.py:61
  520.3 1.2 copy-start.8
  521.6 0.9 copy-start.9
  526.9 207.1 %all-reduce.14.cloned.1.call-start = ((), (), s32[]{:S(2)}) async-start(), calls=%async_computation.3 | async-start | bytes 311296 | tf_op jit(solution)/shard_map/psum | solution.py:61
  592.4 0.7 copy-start.13
  733.9 1.2 copy-start.7
  740.8 0.7 copy-start.4
Sparse Core Ops, SparseCore 0:
  18.6 260.5 all-reduce.15
  284.1 61.9 all-reduce.7
  383.2 137.1 all-reduce.9
  527.0 65.3 all-reduce.11
  595.7 138.1 all-reduce.13
